TPU v7x, 32 devices: a whole 2x2x4 slice. The times are simulated.
32 devices in a mesh: slab: 8 (over z, y), patch: 4 (over x, core).
Axes of the slice: x: 2, y: 2, z: 4, core: 2. Of those that a mesh axis runs over, the one named last changes fastest.
Arguments:
- fluid_state: float32 [16, 256, 256], P('slab', 'patch'), may hold values from -6 to 6
- fluid_rhs: float32 [16, 256, 256], P('slab', 'patch'), may hold values from -24 to 24
- element_scale: float32 [16, 256], P('slab', 'patch'), may hold values from 1 to 4
- element_matrix: bfloat16 [256, 256], replicated
- couple_x: bfloat16 [256, 256], replicated, may hold values from -0.09375 to 0.09375
- couple_y: bfloat16 [256, 256], replicated, may hold values from -0.09375 to 0.09375
- block_inverse: bfloat16 [256, 256], replicated
- traction_map: bfloat16 [3, 256], replicated, may hold values from -0.375 to 0.375
- slot_elem: int32 [8, 4, 1024], P('slab', 'patch'), may hold values from 0 to 127
- slot_point: int32 [8, 4, 1024], P('slab', 'patch'), may hold values from 0 to 8191
- slot_count: int32 [8, 4, 4], P('slab', 'patch'), may hold values from 0 to 256, as said below
- displacement: float32 [3, 256, 128], P(None, 'patch'), may hold values from -6 to 6
- stiffness: float32 [256, 128], P('patch'), may hold values from 0.03 to 0.3
Outputs:
- fluid_out: float32 [16, 256, 256], P('slab', 'patch')
- displacement_new: float32 [3, 256, 128], P(None, 'patch')
- wall_motion: float32 [3, 8, 4, 1024], P(None, 'slab', 'patch')
Inputs may be any that keep to these rules, and one draw needn't show every extreme that they name: For every block and owner only the first slot_count slots of that owner's 256 slots are live; the count 256 is reached for some block and owner in every draw.
All inputs are finite; a program needn't handle non-finite values.
Results may differ from a plain program's by a relative error of at most 0.0049.
Values may be sent and summed in bfloat16 or wider, within the bound.
A program may use at most 128 MiB of HBM per device.

v0:
```python
import jax
import jax.numpy as jnp
from jax import lax
from jax.sharding import PartitionSpec as P

SWEEPS = 3


def with_halo(cells, sides, width):
    for axis, dim in sides:
        count = lax.axis_size(axis)
        ends = count - 1
        head = lax.slice_in_dim(cells, 0, width, axis=dim)
        tail = lax.slice_in_dim(cells, cells.shape[dim] - width, cells.shape[dim], axis=dim)
        cells = jnp.concatenate(
            [
                lax.ppermute(tail, axis, [(i, (i + 1) % count) for i in range(ends)]),
                cells,
                lax.ppermute(head, axis, [((i + 1) % count, i) for i in range(ends)]),
            ],
            axis=dim,
        )
    return cells


def element_apply(rounded, scale, element_matrix, couple_x, couple_y):
    padded = with_halo(rounded, (("slab", 0), ("patch", 1)), 1)
    along_x = (padded[:-2, 1:-1].astype(jnp.float32) + padded[2:, 1:-1].astype(jnp.float32)).astype(
        jnp.bfloat16
    )
    along_y = (padded[1:-1, :-2].astype(jnp.float32) + padded[1:-1, 2:].astype(jnp.float32)).astype(
        jnp.bfloat16
    )
    width = rounded.shape[2]
    own = jnp.dot(rounded.reshape(-1, width), element_matrix, preferred_element_type=jnp.float32)
    side_x = jnp.dot(along_x.reshape(-1, width), couple_x, preferred_element_type=jnp.float32)
    side_y = jnp.dot(along_y.reshape(-1, width), couple_y, preferred_element_type=jnp.float32)
    return (
        scale[:, :, None] * own.reshape(rounded.shape)
        - side_x.reshape(rounded.shape)
        - side_y.reshape(rounded.shape)
    )


def laplace_net(field):
    edged = with_halo(field.astype(jnp.bfloat16), (("patch", 1),), 1).astype(field.dtype)
    edged = jnp.pad(edged, ((0, 0), (0, 0), (1, 1)))
    return 4.0 * field - (
        edged[:, 2:, 1:-1] + edged[:, :-2, 1:-1] + edged[:, 1:-1, 2:] + edged[:, 1:-1, :-2]
    )


def shards(
    fluid_state,
    fluid_rhs,
    element_scale,
    element_matrix,
    couple_x,
    couple_y,
    block_inverse,
    traction_map,
    slot_elem,
    slot_point,
    slot_count,
    displacement,
    stiffness,
):
    width = fluid_state.shape[2]
    state = fluid_state
    for sweep in range(SWEEPS):
        rounded = state.astype(jnp.bfloat16)
        applied = element_apply(rounded, element_scale, element_matrix, couple_x, couple_y)
        residue = (fluid_rhs - applied).astype(jnp.bfloat16)
        update = jnp.dot(
            residue.reshape(-1, width), block_inverse, preferred_element_type=jnp.float32
        ).reshape(state.shape)
        state = state + update / element_scale[:, :, None]
    final = state.astype(jnp.bfloat16)
    owners = lax.axis_size("patch")
    capacity = slot_elem.shape[2] // owners
    net_rows = displacement.shape[1]
    net_cols = displacement.shape[2]
    cells = net_rows * net_cols
    rows = jnp.take(final.reshape(-1, width), slot_elem.reshape(-1), axis=0).reshape(
        owners, capacity, width
    )
    pull = jnp.einsum("cd,kqd->kcq", traction_map, rows, preferred_element_type=jnp.float32)
    limits = slot_count.reshape(owners)
    live = (lax.broadcasted_iota(jnp.int32, (owners, capacity), 1) < limits[:, None]).astype(
        jnp.float32
    )
    pull = pull * live[:, None, :]
    points = slot_point.reshape(owners, capacity)
    owner_ids = lax.broadcasted_iota(jnp.int32, (owners, capacity), 0)
    got_pull, got_points = (
        lax.all_to_all(pull, "patch", split_axis=0, concat_axis=0, tiled=True),
        lax.all_to_all(points, "patch", split_axis=0, concat_axis=0, tiled=True),
    )
    local = jnp.zeros((3, cells), jnp.float32)
    local = local.at[:, got_points.reshape(-1)].add(got_pull.transpose(1, 0, 2).reshape(3, -1))
    loads = lax.psum(local, "slab")
    loads = loads.reshape(3, net_rows, net_cols)
    bend = laplace_net(displacement)
    stiff_term = stiffness[None] * (laplace_net(bend) + 4.0 * bend)
    displacement_new = displacement + (loads - stiff_term) / (36.0 * stiffness[None])
    flat_net = displacement_new.reshape(3, -1)
    whole = lax.all_gather(flat_net, "patch", axis=1, tiled=True)
    picked = whole[:, (owner_ids * cells + points).reshape(-1)]
    wall_motion = (picked * live.reshape(1, -1)).reshape(3, 1, 1, owners * capacity)
    return (state, displacement_new, wall_motion)


def solution(mesh):
    return jax.shard_map(
        shards,
        mesh=mesh,
        in_specs=(
            P("slab", "patch", None),
            P("slab", "patch", None),
            P("slab", "patch"),
            P(),
            P(),
            P(),
            P(),
            P(),
            P("slab", "patch", None),
            P("slab", "patch", None),
            P("slab", "patch", None),
            P(None, "patch", None),
            P("patch", None),
        ),
        out_specs=(
            P("slab", "patch", None),
            P(None, "patch", None),
            P(None, "slab", "patch", None),
        ),
        check_vma=False,
    )
```

profile of v0, /device:TPU:0, one launch (start us, length us, event | category | flops | bytes accessed | tf_op | source)
XLA Modules:
  0.0 299.1 jit_solution(18253544204650045127)
XLA Ops:
  7.2 1.0 convert_element_type.106
  8.3 1.3 collective-permute-start.1
  9.6 5.5 %collective-permute-start = (bf16[1,64,256]{2,1,0:T(8,128)(2,1)S(1)}, bf16[1,64,256]{2,1,0:T(8,128)(2,1)S(1)}, u32[]{:S(2)}, u32[]{:S(2)}) collective-permute-start(bf16[1,64,256]{2,1,0:T(8,128)(2,1)S(1)} %get-tuple-element.24), channel_id=1, source_target_pairs={{0,4},{4,8},{8,12},{12,16},{16,20},{20,24},{24,28},{1,5},{5,9},{9,... | collective-permute-start | bytes 98312 | tf_op jit(solution)/shard_map/ppermute | solution.py:17
  15.1 3.3 %all-to-all-start = ((s32[4,1,256]{2,1,0:T(1,128)}), s32[4,1,256]{2,1,0:T(1,128)S(1)}, u32[]{:S(2)}, u32[]{:S(2)}) async-start(s32[4,1,256]{2,1,0:T(1,128)} %bitcast.90), calls=%async_computation | async-start | bytes 8192 | tf_op jit(solution)/shard_map/all_to_all | solution.py:97
  18.4 0.9 convert_element_type.132
  19.3 1.3 collective-permute-start.13
  20.6 3.0 %collective-permute-start.12 = (bf16[3,1,128]{2,1,0:T(2,128)(2,1)S(1)}, bf16[3,1,128]{2,1,0:T(2,128)(2,1)S(1)}, u32[]{:S(2)}, u32[]{:S(2)}) collective-permute-start(bf16[3,1,128]{2,1,0:T(2,128)(2,1)S(1)} %get-tuple-element.28), channel_id=1, source_target_pairs={{0,1},{1,2},{2,3},{4,5},{5,6},{6,7},{8,9},{9,10},{10,11},{12,13},{... | collective-permute-start | bytes 2312 | tf_op jit(solution)/shard_map/ppermute | solution.py:17
  23.7 0.7 compare_select_fusion.1
  24.4 0.5 broadcast.126
  24.9 1.3 reduce.3
  26.2 0.8 broadcast_multiply_fusion
  27.1 0.7 compare_select_fusion
  27.8 1.1 convolution_multiply_fusion.2
  28.8 0.7 fusion.59
  29.6 1.0 fusion.70
  30.7 1.3 collective-permute-start.15
  32.0 4.3 %collective-permute-start.14 = (bf16[3,1,128]{2,1,0:T(2,128)(2,1)S(1)}, bf16[3,1,128]{2,1,0:T(2,128)(2,1)S(1)}, u32[]{:S(2)}, u32[]{:S(2)}) collective-permute-start(bf16[3,1,128]{2,1,0:T(2,128)(2,1)S(1)} %get-tuple-element.26), channel_id=1, source_target_pairs={{0,1},{1,2},{2,3},{4,5},{5,6},{6,7},{8,9},{9,10},{10,11},{12,13},{... | collective-permute-start | bytes 2312 | tf_op jit(solution)/shard_map/ppermute | solution.py:17
  36.3 1.3 collective-permute-start.3
  37.6 4.3 %collective-permute-start.2 = (bf16[4,1,256]{2,1,0:T(2,128)(2,1)S(1)}, bf16[4,1,256]{2,1,0:T(2,128)(2,1)S(1)}, u32[]{:S(2)}, u32[]{:S(2)}) collective-permute-start(bf16[4,1,256]{2,1,0:T(2,128)(2,1)S(1)} %get-tuple-element.18), channel_id=1, source_target_pairs={{0,1},{1,2},{2,3},{4,5},{5,6},{6,7},{8,9},{9,10},{10,11},{12,13},{... | collective-permute-start | bytes 6152 | tf_op jit(solution)/shard_map/ppermute | solution.py:17
  41.9 1.1 convolution_subtract_fusion.5
  43.0 1.3 fusion.77
  44.3 1.3 collective-permute-start.5
  45.6 5.4 %collective-permute-start.4 = (bf16[1,64,256]{2,1,0:T(8,128)(2,1)S(1)}, bf16[1,64,256]{2,1,0:T(8,128)(2,1)S(1)}, u32[]{:S(2)}, u32[]{:S(2)}) collective-permute-start(bf16[1,64,256]{2,1,0:T(8,128)(2,1)S(1)} %get-tuple-element.22), channel_id=1, source_target_pairs={{0,4},{4,8},{8,12},{12,16},{16,20},{20,24},{24,28},{1,5},{5,9},{9,... | collective-permute-start | bytes 98312 | tf_op jit(solution)/shard_map/ppermute | solution.py:17
  51.1 1.1 convolution_multiply_fusion.1
  52.1 0.5 collective-permute-done.4
  52.6 1.3 collective-permute-start.7
  53.9 3.5 %collective-permute-start.6 = (bf16[4,1,256]{2,1,0:T(2,128)(2,1)S(1)}, bf16[4,1,256]{2,1,0:T(2,128)(2,1)S(1)}, u32[]{:S(2)}, u32[]{:S(2)}) collective-permute-start(bf16[4,1,256]{2,1,0:T(2,128)(2,1)S(1)} %get-tuple-element.16), channel_id=1, source_target_pairs={{0,1},{1,2},{2,3},{4,5},{5,6},{6,7},{8,9},{9,10},{10,11},{12,13},{... | collective-permute-start | bytes 6152 | tf_op jit(solution)/shard_map/ppermute | solution.py:17
  57.7 0.6 collective-permute-done.6
  58.3 0.3 fusion.80
  58.6 1.3 collective-permute-start.9
  59.9 5.2 %collective-permute-start.8 = (bf16[1,64,256]{2,1,0:T(8,128)(2,1)S(1)}, bf16[1,64,256]{2,1,0:T(8,128)(2,1)S(1)}, u32[]{:S(2)}, u32[]{:S(2)}) collective-permute-start(bf16[1,64,256]{2,1,0:T(8,128)(2,1)S(1)} %get-tuple-element.20), channel_id=1, source_target_pairs={{0,4},{4,8},{8,12},{12,16},{16,20},{20,24},{24,28},{1,5},{5,9},{9,... | collective-permute-start | bytes 98312 | tf_op jit(solution)/shard_map/ppermute | solution.py:17
  65.3 1.4 collective-permute-done.8
  66.7 1.3 collective-permute-start.11
  68.0 4.5 %collective-permute-start.10 = (bf16[4,1,256]{2,1,0:T(2,128)(2,1)S(1)}, bf16[4,1,256]{2,1,0:T(2,128)(2,1)S(1)}, u32[]{:S(2)}, u32[]{:S(2)}) collective-permute-start(bf16[4,1,256]{2,1,0:T(2,128)(2,1)S(1)} %get-tuple-element.14), channel_id=1, source_target_pairs={{0,1},{1,2},{2,3},{4,5},{5,6},{6,7},{8,9},{9,10},{10,11},{12,13},{... | collective-permute-start | bytes 6152 | tf_op jit(solution)/shard_map/ppermute | solution.py:17
  72.7 0.6 collective-permute-done.10
  73.3 1.0 fusion.83
  74.3 3.9 %gather_fusion = bf16[1024,256]{1,0:T(8,128)(2,1)S(1)} fusion(bf16[128,256]{1,0:T(8,128)(2,1)S(1)} %bitcast.84, s32[1024]{0:T(1024)S(1)} %broadcast_clamp_fusion.1), kind=kCustom, calls=%fused_computation | custom fusion | bytes 1052672 | tf_op jit(solution)/shard_map/jit(_take)/gather | solution.py:84
  78.3 0.9 fusion.11
  79.2 6.5 %all-to-all-start.1 = ((f32[4,3,256]{2,1,0:T(4,128)}), f32[4,3,256]{2,1,0:T(4,128)S(1)}, u32[]{:S(2)}, u32[]{:S(2)}) async-start(f32[4,3,256]{2,1,0:T(4,128)} %fusion.11), calls=%async_computation.1 | async-start | bytes 32768 | tf_op jit(solution)/shard_map/all_to_all | solution.py:96
  85.7 3.8 %all-to-all-done.1 = f32[4,3,256]{2,1,0:T(4,128)S(1)} async-done(((f32[4,3,256]{2,1,0:T(4,128)}), f32[4,3,256]{2,1,0:T(4,128)S(1)}, u32[]{:S(2)}, u32[]{:S(2)}) %all-to-all-start.1) | async-done | bytes 12320 | tf_op jit(solution)/shard_map/all_to_all | solution.py:96
  89.8 8.2 %scatter_custom_fusion = f32[3,8192]{0,1:T(8,128)} fusion(s32[1024]{0:T(1024)S(1)} %bitcast.95, f32[1024,3]{1,0:T(8,128)S(1)} %copy.23, f32[]{:T(128)} %constant.9.clone.1), kind=kCustom, calls=%fused_computation.3 | custom fusion | flops 3072 | bytes 98308 | tf_op jit(solution)/shard_map/scatter-add | solution.py:100
  98.0 3.5 %copy.24 = f32[3,64,128]{2,1,0:T(8,128)} copy(f32[3,64,128]{0,2,1:T(8,128)} %bitcast.86) | data formatting | bytes 196608 | tf_op jit(solution)/shard_map/reshape | solution.py:102
  101.6 73.6 %all-reduce.4.cloned.1.call-done = f32[3,64,128]{2,1,0:T(8,128)} async-done(((f32[3,64,128]{2,1,0:T(8,128)}), f32[3,64,128]{2,1,0:T(8,128)}) %all-reduce.4.cloned.1.call-update) | async-done | bytes 98320 | tf_op jit(solution)/shard_map/psum | solution.py:101
  175.2 1.0 fusion.33
  176.2 2.6 copy.25
  178.8 103.9 %all_gather.3 = f32[3,32768]{0,1:T(8,128)} all-gather(f32[3,8192]{0,1:T(8,128)} %bitcast.85), channel_id=1, replica_groups=mesh['slab'=8,'patch'=4] {'patch'}, dimensions={1}, use_global_device_ids=true | all-gather | bytes 491520 | tf_op jit(solution)/shard_map/all_gather | solution.py:107
  282.7 8.6 %gather_fusion.1 = f32[1024,3]{1,0:T(8,128)S(1)} fusion(f32[3,32768]{0,1:T(8,128)} %all_gather.3, s32[1024]{0:T(1024)S(1)} %broadcast_clamp_fusion), kind=kCustom, calls=%fused_computation.1 | custom fusion | bytes 28672 | tf_op jit(solution)/shard_map/gather | solution.py:108
  291.5 0.8 copy.26
  (58 shorter events, 1.3 us)
Async XLA Ops:
  7.2 35.8 %copy-start = (bf16[256,256]{1,0:T(8,128)(2,1)S(1)}, bf16[256,256]{1,0:T(8,128)(2,1)}, u32[]{:S(2)}) copy-start(bf16[256,256]{1,0:T(8,128)(2,1)} %param.19) | copy-start | bytes 393220
  7.2 51.1 %copy-start.6 = (f32[2,64]{1,0:T(2,128)S(1)}, f32[2,64]{1,0:T(2,128)}, u32[]{:S(2)}) copy-start(f32[2,64]{1,0:T(2,128)} %param.15) | copy-start | bytes 1540
  7.2 57.9 %copy-start.1 = (bf16[256,256]{1,0:T(8,128)(2,1)S(1)}, bf16[256,256]{1,0:T(8,128)(2,1)}, u32[]{:S(2)}) copy-start(bf16[256,256]{1,0:T(8,128)(2,1)} %param.16) | copy-start | bytes 393220
  7.2 50.3 %copy-start.2 = (bf16[256,256]{1,0:T(8,128)(2,1)S(1)}, bf16[256,256]{1,0:T(8,128)(2,1)}, u32[]{:S(2)}) copy-start(bf16[256,256]{1,0:T(8,128)(2,1)} %param.17) | copy-start | bytes 393220
  7.2 51.1 %copy-start.7 = (f32[2,64,256]{2,1,0:T(8,128)S(1)}, f32[2,64,256]{2,1,0:T(8,128)}, u32[]{:S(2)}) copy-start(f32[2,64,256]{2,1,0:T(8,128)} %param.14) | copy-start | bytes 393220
  7.2 51.1 %copy-start.8 = (bf16[256,256]{1,0:T(8,128)(2,1)S(1)}, bf16[256,256]{1,0:T(8,128)(2,1)}, u32[]{:S(2)}) copy-start(bf16[256,256]{1,0:T(8,128)(2,1)} %param.18) | copy-start | bytes 393220
  8.3 28.0 %collective-permute-start.1 = (bf16[1,64,256]{2,1,0:T(8,128)(2,1)S(1)}, bf16[1,64,256]{2,1,0:T(8,128)(2,1)S(1)}, u32[]{:S(2)}, u32[]{:S(2)}) collective-permute-start(bf16[1,64,256]{2,1,0:T(8,128)(2,1)S(1)} %get-tuple-element.25), channel_id=1, source_target_pairs={{4,0},{8,4},{12,8},{16,12},{20,16},{24,20},{28,24},{5,1},{9,5},{13... | collective-permute-start | bytes 98312 | tf_op jit(solution)/shard_map/ppermute | solution.py:19
  9.6 26.7 %collective-permute-start = (bf16[1,64,256]{2,1,0:T(8,128)(2,1)S(1)}, bf16[1,64,256]{2,1,0:T(8,128)(2,1)S(1)}, u32[]{:S(2)}, u32[]{:S(2)}) collective-permute-start(bf16[1,64,256]{2,1,0:T(8,128)(2,1)S(1)} %get-tuple-element.24), channel_id=1, source_target_pairs={{0,4},{4,8},{8,12},{12,16},{16,20},{20,24},{24,28},{1,5},{5,9},{9,... | collective-permute-start | bytes 98312 | tf_op jit(solution)/shard_map/ppermute | solution.py:17
  15.1 64.1 %all-to-all-start = ((s32[4,1,256]{2,1,0:T(1,128)}), s32[4,1,256]{2,1,0:T(1,128)S(1)}, u32[]{:S(2)}, u32[]{:S(2)}) async-start(s32[4,1,256]{2,1,0:T(1,128)} %bitcast.90), calls=%async_computation | async-start | bytes 8192 | tf_op jit(solution)/shard_map/all_to_all | solution.py:97
  19.3 10.3 %collective-permute-start.13 = (bf16[3,1,128]{2,1,0:T(2,128)(2,1)S(1)}, bf16[3,1,128]{2,1,0:T(2,128)(2,1)S(1)}, u32[]{:S(2)}, u32[]{:S(2)}) collective-permute-start(bf16[3,1,128]{2,1,0:T(2,128)(2,1)S(1)} %get-tuple-element.29), channel_id=1, source_target_pairs={{1,0},{2,1},{3,2},{5,4},{6,5},{7,6},{9,8},{10,9},{11,10},{13,12},{... | collective-permute-start | bytes 2312 | tf_op jit(solution)/shard_map/ppermute | solution.py:19
  20.6 9.0 %collective-permute-start.12 = (bf16[3,1,128]{2,1,0:T(2,128)(2,1)S(1)}, bf16[3,1,128]{2,1,0:T(2,128)(2,1)S(1)}, u32[]{:S(2)}, u32[]{:S(2)}) collective-permute-start(bf16[3,1,128]{2,1,0:T(2,128)(2,1)S(1)} %get-tuple-element.28), channel_id=1, source_target_pairs={{0,1},{1,2},{2,3},{4,5},{5,6},{6,7},{8,9},{9,10},{10,11},{12,13},{... | collective-permute-start | bytes 2312 | tf_op jit(solution)/shard_map/ppermute | solution.py:17
  30.7 70.8 %collective-permute-start.15 = (bf16[3,1,128]{2,1,0:T(2,128)(2,1)S(1)}, bf16[3,1,128]{2,1,0:T(2,128)(2,1)S(1)}, u32[]{:S(2)}, u32[]{:S(2)}) collective-permute-start(bf16[3,1,128]{2,1,0:T(2,128)(2,1)S(1)} %get-tuple-element.27), channel_id=1, source_target_pairs={{1,0},{2,1},{3,2},{5,4},{6,5},{7,6},{9,8},{10,9},{11,10},{13,12},{... | collective-permute-start | bytes 2312 | tf_op jit(solution)/shard_map/ppermute | solution.py:19
  32.0 69.6 %collective-permute-start.14 = (bf16[3,1,128]{2,1,0:T(2,128)(2,1)S(1)}, bf16[3,1,128]{2,1,0:T(2,128)(2,1)S(1)}, u32[]{:S(2)}, u32[]{:S(2)}) collective-permute-start(bf16[3,1,128]{2,1,0:T(2,128)(2,1)S(1)} %get-tuple-element.26), channel_id=1, source_target_pairs={{0,1},{1,2},{2,3},{4,5},{5,6},{6,7},{8,9},{9,10},{10,11},{12,13},{... | collective-permute-start | bytes 2312 | tf_op jit(solution)/shard_map/ppermute | solution.py:17
  36.3 6.7 %collective-permute-start.3 = (bf16[4,1,256]{2,1,0:T(2,128)(2,1)S(1)}, bf16[4,1,256]{2,1,0:T(2,128)(2,1)S(1)}, u32[]{:S(2)}, u32[]{:S(2)}) collective-permute-start(bf16[4,1,256]{2,1,0:T(2,128)(2,1)S(1)} %get-tuple-element.19), channel_id=1, source_target_pairs={{1,0},{2,1},{3,2},{5,4},{6,5},{7,6},{9,8},{10,9},{11,10},{13,12},{... | collective-permute-start | bytes 6152 | tf_op jit(solution)/shard_map/ppermute | solution.py:19
  37.6 5.4 %collective-permute-start.2 = (bf16[4,1,256]{2,1,0:T(2,128)(2,1)S(1)}, bf16[4,1,256]{2,1,0:T(2,128)(2,1)S(1)}, u32[]{:S(2)}, u32[]{:S(2)}) collective-permute-start(bf16[4,1,256]{2,1,0:T(2,128)(2,1)S(1)} %get-tuple-element.18), channel_id=1, source_target_pairs={{0,1},{1,2},{2,3},{4,5},{5,6},{6,7},{8,9},{9,10},{10,11},{12,13},{... | collective-permute-start | bytes 6152 | tf_op jit(solution)/shard_map/ppermute | solution.py:17
  44.3 7.8 %collective-permute-start.5 = (bf16[1,64,256]{2,1,0:T(8,128)(2,1)S(1)}, bf16[1,64,256]{2,1,0:T(8,128)(2,1)S(1)}, u32[]{:S(2)}, u32[]{:S(2)}) collective-permute-start(bf16[1,64,256]{2,1,0:T(8,128)(2,1)S(1)} %get-tuple-element.23), channel_id=1, source_target_pairs={{4,0},{8,4},{12,8},{16,12},{20,16},{24,20},{28,24},{5,1},{9,5},{13... | collective-permute-start | bytes 98312 | tf_op jit(solution)/shard_map/ppermute | solution.py:19
  45.6 7.0 %collective-permute-start.4 = (bf16[1,64,256]{2,1,0:T(8,128)(2,1)S(1)}, bf16[1,64,256]{2,1,0:T(8,128)(2,1)S(1)}, u32[]{:S(2)}, u32[]{:S(2)}) collective-permute-start(bf16[1,64,256]{2,1,0:T(8,128)(2,1)S(1)} %get-tuple-element.22), channel_id=1, source_target_pairs={{0,4},{4,8},{8,12},{12,16},{16,20},{20,24},{24,28},{1,5},{5,9},{9,... | collective-permute-start | bytes 98312 | tf_op jit(solution)/shard_map/ppermute | solution.py:17
  52.6 5.0 %collective-permute-start.7 = (bf16[4,1,256]{2,1,0:T(2,128)(2,1)S(1)}, bf16[4,1,256]{2,1,0:T(2,128)(2,1)S(1)}, u32[]{:S(2)}, u32[]{:S(2)}) collective-permute-start(bf16[4,1,256]{2,1,0:T(2,128)(2,1)S(1)} %get-tuple-element.17), channel_id=1, source_target_pairs={{1,0},{2,1},{3,2},{5,4},{6,5},{7,6},{9,8},{10,9},{11,10},{13,12},{... | collective-permute-start | bytes 6152 | tf_op jit(solution)/shard_map/ppermute | solution.py:19
  53.9 4.3 %collective-permute-start.6 = (bf16[4,1,256]{2,1,0:T(2,128)(2,1)S(1)}, bf16[4,1,256]{2,1,0:T(2,128)(2,1)S(1)}, u32[]{:S(2)}, u32[]{:S(2)}) collective-permute-start(bf16[4,1,256]{2,1,0:T(2,128)(2,1)S(1)} %get-tuple-element.16), channel_id=1, source_target_pairs={{0,1},{1,2},{2,3},{4,5},{5,6},{6,7},{8,9},{9,10},{10,11},{12,13},{... | collective-permute-start | bytes 6152 | tf_op jit(solution)/shard_map/ppermute | solution.py:17
  57.6 20.6 %copy-start.9 = (bf16[3,256]{1,0:T(4,128)(2,1)S(1)}, bf16[3,256]{1,0:T(4,128)(2,1)}, u32[]{:S(2)}) copy-start(bf16[3,256]{1,0:T(4,128)(2,1)} %param.20) | copy-start | bytes 4612
  58.6 6.7 %collective-permute-start.9 = (bf16[1,64,256]{2,1,0:T(8,128)(2,1)S(1)}, bf16[1,64,256]{2,1,0:T(8,128)(2,1)S(1)}, u32[]{:S(2)}, u32[]{:S(2)}) collective-permute-start(bf16[1,64,256]{2,1,0:T(8,128)(2,1)S(1)} %get-tuple-element.21), channel_id=1, source_target_pairs={{4,0},{8,4},{12,8},{16,12},{20,16},{24,20},{28,24},{5,1},{9,5},{13... | collective-permute-start | bytes 98312 | tf_op jit(solution)/shard_map/ppermute | solution.py:19
  59.9 6.8 %collective-permute-start.8 = (bf16[1,64,256]{2,1,0:T(8,128)(2,1)S(1)}, bf16[1,64,256]{2,1,0:T(8,128)(2,1)S(1)}, u32[]{:S(2)}, u32[]{:S(2)}) collective-permute-start(bf16[1,64,256]{2,1,0:T(8,128)(2,1)S(1)} %get-tuple-element.20), channel_id=1, source_target_pairs={{0,4},{4,8},{8,12},{12,16},{16,20},{20,24},{24,28},{1,5},{5,9},{9,... | collective-permute-start | bytes 98312 | tf_op jit(solution)/shard_map/ppermute | solution.py:17
  66.7 6.0 %collective-permute-start.11 = (bf16[4,1,256]{2,1,0:T(2,128)(2,1)S(1)}, bf16[4,1,256]{2,1,0:T(2,128)(2,1)S(1)}, u32[]{:S(2)}, u32[]{:S(2)}) collective-permute-start(bf16[4,1,256]{2,1,0:T(2,128)(2,1)S(1)} %get-tuple-element.15), channel_id=1, source_target_pairs={{1,0},{2,1},{3,2},{5,4},{6,5},{7,6},{9,8},{10,9},{11,10},{13,12},{... | collective-permute-start | bytes 6152 | tf_op jit(solution)/shard_map/ppermute | solution.py:19
  68.0 5.4 %collective-permute-start.10 = (bf16[4,1,256]{2,1,0:T(2,128)(2,1)S(1)}, bf16[4,1,256]{2,1,0:T(2,128)(2,1)S(1)}, u32[]{:S(2)}, u32[]{:S(2)}) collective-permute-start(bf16[4,1,256]{2,1,0:T(2,128)(2,1)S(1)} %get-tuple-element.14), channel_id=1, source_target_pairs={{0,1},{1,2},{2,3},{4,5},{5,6},{6,7},{8,9},{9,10},{10,11},{12,13},{... | collective-permute-start | bytes 6152 | tf_op jit(solution)/shard_map/ppermute | solution.py:17
  79.2 10.4 %all-to-all-start.1 = ((f32[4,3,256]{2,1,0:T(4,128)}), f32[4,3,256]{2,1,0:T(4,128)S(1)}, u32[]{:S(2)}, u32[]{:S(2)}) async-start(f32[4,3,256]{2,1,0:T(4,128)} %fusion.11), calls=%async_computation.1 | async-start | bytes 32768 | tf_op jit(solution)/shard_map/all_to_all | solution.py:96
  85.7 89.5 %all-reduce.4.cloned.1.call-start = ((), (), s32[]{:S(2)}) async-start(), calls=%async_computation.2 | async-start | bytes 196608 | tf_op jit(solution)/shard_map/psum | solution.py:101
  89.8 85.4 %copy-start.3 = (f32[3,64,128]{2,1,0:T(8,128)S(1)}, f32[3,64,128]{2,1,0:T(8,128)}, u32[]{:S(2)}) copy-start(f32[3,64,128]{2,1,0:T(8,128)} %param.24) | copy-start | bytes 294916
  89.8 85.4 %copy-start.5 = (f32[64,128]{1,0:T(8,128)S(1)}, f32[64,128]{1,0:T(8,128)}, u32[]{:S(2)}) copy-start(f32[64,128]{1,0:T(8,128)} %param.25) | copy-start | bytes 98308
  176.2 106.5 %copy-start.4 = (f32[3,64,128]{2,1,0:T(8,128)}, f32[3,64,128]{2,1,0:T(8,128)S(1)}, u32[]{:S(2)}) copy-start(f32[3,64,128]{2,1,0:T(8,128)S(1)} %fusion.33) | copy-start | bytes 294916
Sparse Core Ops, SparseCore 0:
  101.6 73.4 all-reduce.3
where the time goes:
time: 300 us; the launch traced here: 299 us
  blocking collectives  104 us (35%)
  waiting for transfers between devices  80.6 us (27%)
  starting transfers between devices  55.9 us (19%)
  local copies, waits for them, and re-layouts  20.3 us (7%)
  other arithmetic  16.7 us (6%)
  between operations  14.5 us (5%)
  matrix products  7.25 us (2%)
    all_gather x1, blocking collectives, shards(): whole = lax.all_gather(flat_net, 'patch', axis=1, tiled=True)  104 us
    psum x1, waiting for transfers between devices, shards(): loads = lax.psum(local, 'slab')  73.6 us
    ppermute x8, starting transfers between devices, with_halo(): lax.ppermute(tail, axis, [(i, (i + 1) % count) for i in range(ends)])  35.8 us
    ppermute x8, starting transfers between devices, with_halo(): lax.ppermute(head, axis, [((i + 1) % count, i) for i in range(ends)])  10.3 us
    gather x1, local copies, waits for them, and re-layouts, shards(): picked = whole[:, (owner_ids * cells + points).reshape(-1)]  8.57 us
    scatter-add x1, other arithmetic, shards(): local.at[:, got_points.reshape(-1)]  8.21 us
    all_to_all x1, starting transfers between devices, shards(): lax.all_to_all(pull, 'patch', split_axis=0, concat_axis=0, tiled=True)  6.5 us
  transfers between devices with their start and end apart: 19, of which 6 were waited for; matrix products, arithmetic and copies ran while one was open for 10% of the time, Pallas kernels for 0%

commit v1 on v0

v1 whole, which is shorter than its diff:
```python
import functools

import jax
import jax.numpy as jnp
from jax import lax
from jax.experimental import pallas as pl
from jax.experimental.pallas import tpu as pltpu
from jax.sharding import PartitionSpec as P

SWEEPS = 3
PACK = 16
EDGE = 8
MESH = pl.DeviceIdType.MESH
F32 = jnp.float32
BF16 = jnp.bfloat16


def dot(a, b):
    return jnp.dot(a, b, preferred_element_type=F32)


def dot_nt(a, b):
    return lax.dot_general(a, b, (((1,), (1,)), ((), ())), preferred_element_type=F32)


def split_point(point, cols):
    if cols & (cols - 1) == 0:
        return lax.shift_right_logical(point, cols.bit_length() - 1), point & (cols - 1)
    row = lax.div(point, cols)
    return row, point - row * cols


def column(row_vector):
    n = row_vector.shape[1]
    shape = (n, n)
    eye = lax.broadcasted_iota(jnp.int32, shape, 0) == lax.broadcasted_iota(jnp.int32, shape, 1)
    return jnp.sum(jnp.where(eye, jnp.broadcast_to(row_vector, shape), 0.0), axis=1, keepdims=True)


def laplace(x):
    rows, cols = x.shape
    lane = lax.broadcasted_iota(jnp.int32, x.shape, 1)
    left = jnp.where(lane == 0, 0.0, pltpu.roll(x, 1, 1))
    right = jnp.where(lane == cols - 1, 0.0, pltpu.roll(x, cols - 1, 1))
    return 4.0 * x - (pltpu.roll(x, 1, 0) + pltpu.roll(x, rows - 1, 0) + left + right)


def kernel(
    slabs,
    patches,
    state_ref,
    rhs_ref,
    scale_ref,
    matrix_ref,
    cx_ref,
    cy_ref,
    inverse_ref,
    traction_ref,
    elem_ref,
    point_ref,
    count_ref,
    disp_ref,
    stiff_ref,
    fluid_ref,
    net_ref,
    wall_ref,
    vb,
    halo_x,
    halo_y,
    halo_d,
    points,
    pulls,
    pull_out,
    picks_out,
    picks_in,
    onehot_elem,
    onehot_row,
    onehot_col,
    kd_buf,
    sx,
    rx,
    sy,
    ry,
    sd,
    rd,
    sp1,
    rp1,
    sp2,
    rp2,
    sq1,
    rq1,
    sq2,
    rq2,
    sw,
    rw,
):
    s = lax.axis_index("slab")
    p = lax.axis_index("patch")
    ex, ey, dof = state_ref.shape
    comps, rows, cols = disp_ref.shape
    cap = elem_ref.shape[2] // patches

    def slab_peer(j):
        return lax.rem(s + j, slabs)

    def patch_peer(j):
        return lax.rem(p + j, patches)

    barrier = pltpu.get_barrier_semaphore()
    for j in range(1, slabs):
        pl.semaphore_signal(barrier, inc=1, device_id=(slab_peer(j), p), device_id_type=MESH)
    for j in range(1, patches):
        pl.semaphore_signal(barrier, inc=1, device_id=(s, patch_peer(j)), device_id_type=MESH)

    def remote(src, dst, send, recv, target):
        return pltpu.make_async_remote_copy(
            src_ref=src, dst_ref=dst, send_sem=send, recv_sem=recv, device_id=target, device_id_type=MESH
        )

    def x_up(k):
        return remote(vb.at[k, ex - 1], halo_x.at[k, 0], sx.at[k, 0], rx.at[k, 0], (jnp.minimum(s + 1, slabs - 1), p))

    def x_down(k):
        return remote(vb.at[k, 0], halo_x.at[k, 1], sx.at[k, 1], rx.at[k, 1], (jnp.maximum(s - 1, 0), p))

    def y_up(k):
        return remote(
            vb.at[k, :, pl.ds(ey - PACK, PACK)], halo_y.at[k, 0], sy.at[k, 0], ry.at[k, 0],
            (s, jnp.minimum(p + 1, patches - 1)),
        )

    def y_down(k):
        return remote(
            vb.at[k, :, pl.ds(0, PACK)], halo_y.at[k, 1], sy.at[k, 1], ry.at[k, 1], (s, jnp.maximum(p - 1, 0))
        )

    def d_up():
        return remote(
            disp_ref.at[:, pl.ds(rows - EDGE, EDGE)], halo_d.at[0], sd.at[0], rd.at[0],
            (s, jnp.minimum(p + 1, patches - 1)),
        )

    def d_down():
        return remote(disp_ref.at[:, pl.ds(0, EDGE)], halo_d.at[1], sd.at[1], rd.at[1], (s, jnp.maximum(p - 1, 0)))

    has_prev_s, has_next_s = s > 0, s < slabs - 1
    has_prev_p, has_next_p = p > 0, p < patches - 1

    def point_first(j, mine):
        peer = patch_peer(j)
        src = point_ref.at[0, :, pl.ds(pl.multiple_of(peer * cap, cap), cap)]
        slot = p if mine else peer
        return remote(src, points.at[s, slot], sp1.at[j], rp1.at[slot], (s, peer))

    def point_second(j, mine):
        peer = slab_peer(j)
        slot = s if mine else peer
        return remote(points.at[s], points.at[slot], sp2.at[j], rp2.at[slot], (peer, p))

    def pull_first(j, mine):
        peer = patch_peer(j)
        slot = p if mine else peer
        return remote(pull_out.at[peer], pulls.at[s, slot], sq1.at[j], rq1.at[slot], (s, peer))

    def pull_second(j, mine):
        peer = slab_peer(j)
        slot = s if mine else peer
        return remote(pulls.at[s], pulls.at[slot], sq2.at[j], rq2.at[slot], (peer, p))

    def pick_copy(j, mine):
        peer = patch_peer(j)
        slot = p if mine else peer
        return remote(picks_out.at[peer], picks_in.at[slot], sw.at[j], rw.at[slot], (s, peer))

    def send_halos(k):
        pl.when(has_next_s)(lambda: x_up(k).start())
        pl.when(has_prev_s)(lambda: x_down(k).start())
        pl.when(has_next_p)(lambda: y_up(k).start())
        pl.when(has_prev_p)(lambda: y_down(k).start())

    scales = [column(scale_ref[i : i + 1, :]) for i in range(ex)]
    inverses = [1.0 / x for x in scales]

    def build_points(slab):
        for k in range(patches):
            row, col = split_point(points[slab, k], cols)
            span = pl.ds(k * cap, cap)
            onehot_row[slab, :, span] = jnp.where(
                lax.broadcasted_iota(jnp.int32, (rows, cap), 0) == row, 1.0, 0.0
            ).astype(BF16)
            onehot_col[slab, :, span] = jnp.where(
                lax.broadcasted_iota(jnp.int32, (cols, cap), 0) == col, 1.0, 0.0
            ).astype(BF16)

    def lives(k):
        lane = lax.broadcasted_iota(jnp.int32, (1, cap), 1)
        return lane < count_ref[0, :, k : k + 1]

    def shell():
        pl.when(has_prev_p)(lambda: d_up().wait_recv())
        pl.when(has_next_p)(lambda: d_down().wait_recv())
        total = rows + 2 * EDGE
        line = lax.broadcasted_iota(jnp.int32, (total, cols), 0)
        first = jnp.where(has_prev_p, 0, EDGE)
        last = jnp.where(has_next_p, total, EDGE + rows)
        valid = (line >= first) & (line < last)
        for c in range(comps):
            field = jnp.concatenate([halo_d[0, c], disp_ref[c], halo_d[1, c]], axis=0)
            field = jnp.where(valid, field, 0.0)
            bend = jnp.where(valid, laplace(field), 0.0)
            full = (laplace(bend) + 4.0 * bend)[EDGE : EDGE + rows]
            kd_buf[c] = stiff_ref[...] * full

    v = state_ref[...]
    for k in range(SWEEPS):
        rounded = v.astype(BF16)
        vb[k] = rounded
        if k > 0:
            send_halos(k)
        own = dot(rounded.reshape(ex * ey, dof), matrix_ref[...]).reshape(ex, ey, dof)
        base = [rhs_ref[i] - scales[i] * own[i] for i in range(ex)]
        if k == 0:
            for owner in range(patches):
                elem = elem_ref[0, :, owner * cap : (owner + 1) * cap]
                hit = (lax.broadcasted_iota(jnp.int32, (ex * ey, cap), 0) == elem) & lives(owner)
                onehot_elem[owner] = jnp.where(hit, 1.0, 0.0).astype(BF16)
            for owner in range(patches):

                @pl.when(p == owner)
                def _():
                    points[s, owner] = point_ref[0, :, owner * cap : (owner + 1) * cap]

            pl.semaphore_wait(barrier, slabs - 1 + patches - 1)
            send_halos(0)
            for j in range(1, patches):
                point_first(j, True).start()
            pl.when(has_next_p)(lambda: d_up().start())
            pl.when(has_prev_p)(lambda: d_down().start())
        if k == 1:
            for j in range(1, patches):
                point_first(j, False).wait_recv()
            for j in range(1, slabs):
                point_second(j, True).start()
            build_points(s)
            shell()
        if k == 2:

            def arrive(j, carry):
                point_second(j, False).wait_recv()
                build_points(slab_peer(j))
                return carry

            lax.fori_loop(1, slabs, arrive, 0)

        wide = rounded.astype(F32)
        pl.when(has_prev_p)(lambda: y_up(k).wait_recv())
        pl.when(has_next_p)(lambda: y_down(k).wait_recv())
        line = lax.broadcasted_iota(jnp.int32, (ey, dof), 0)
        along_y = []
        for i in range(ex):
            before = halo_y[k, 0, i].astype(F32)[PACK - 1 : PACK]
            after = halo_y[k, 1, i].astype(F32)[0:1]
            before = jnp.where(has_prev_p, before, 0.0)
            after = jnp.where(has_next_p, after, 0.0)
            prev = jnp.where(line == 0, jnp.broadcast_to(before, (ey, dof)), pltpu.roll(wide[i], 1, 0))
            following = jnp.where(line == ey - 1, jnp.broadcast_to(after, (ey, dof)), pltpu.roll(wide[i], ey - 1, 0))
            along_y.append((prev + following).astype(BF16))
        side_y = dot(jnp.concatenate(along_y, axis=0), cy_ref[...])
        pl.when(has_prev_s)(lambda: x_up(k).wait_recv())
        pl.when(has_next_s)(lambda: x_down(k).wait_recv())
        low = jnp.where(has_prev_s, halo_x[k, 0].astype(F32), 0.0)
        high = jnp.where(has_next_s, halo_x[k, 1].astype(F32), 0.0)
        along_x = []
        for i in range(ex):
            below = low if i == 0 else wide[i - 1]
            above = high if i == ex - 1 else wide[i + 1]
            along_x.append((below + above).astype(BF16))
        side_x = dot(jnp.concatenate(along_x, axis=0), cx_ref[...])
        side = (side_x + side_y).reshape(ex, ey, dof)
        residue = jnp.concatenate([(base[i] + side[i]).astype(BF16) for i in range(ex)], axis=0)
        update = dot(residue, inverse_ref[...]).reshape(ex, ey, dof)
        v = jnp.stack([v[i] + update[i] * inverses[i] for i in range(ex)], axis=0)

    final = v.astype(BF16).reshape(ex * ey, dof)
    traction = dot_nt(traction_ref[...], final).astype(BF16)
    for owner in range(patches):
        pull_out[owner] = dot(traction, onehot_elem[owner]).astype(BF16)
    for j in range(1, patches):
        pull_first(j, True).start()
    pulls[s, p] = pull_out[p]
    fluid_ref[...] = v
    for j in range(1, patches):
        pull_first(j, False).wait_recv()
    for j in range(1, slabs):
        pull_second(j, True).start()

    def scatter(slab, acc):
        for k in range(patches):
            span = pl.ds(k * cap, cap)
            hot = onehot_row[slab, :, span]
            value = pulls[slab, k]
            scaled = jnp.concatenate([hot * value[c : c + 1] for c in range(comps)], axis=0)
            acc = acc + dot_nt(scaled, onehot_col[slab, :, span])
        return acc

    acc = scatter(s, jnp.zeros((comps * rows, cols), F32))

    def gathered(j, acc):
        pull_second(j, False).wait_recv()
        return scatter(slab_peer(j), acc)

    acc = lax.fori_loop(1, slabs, gathered, acc)
    loads = acc.reshape(comps, rows, cols)
    gain = 1.0 / (36.0 * stiff_ref[...])
    fresh = [disp_ref[c] + (loads[c] - kd_buf[c]) * gain for c in range(comps)]
    narrow = jnp.concatenate([x.astype(BF16) for x in fresh], axis=0)
    for k in range(patches):
        span = pl.ds(k * cap, cap)
        spread = dot(narrow, onehot_col[s, :, span]).reshape(comps, rows, cap)
        hot = onehot_row[s, :, span].astype(F32)
        for c in range(comps):
            picks_out[k, c : c + 1] = jnp.sum(spread[c] * hot, axis=0, keepdims=True)
    for j in range(1, patches):
        pick_copy(j, True).start()
    picks_in[p] = picks_out[p]
    for c in range(comps):
        net_ref[c] = fresh[c]
    for j in range(1, patches):
        pick_copy(j, False).wait_recv()
    for k in range(patches):
        live = lives(k)
        for c in range(comps):
            wall_ref[c, 0, :, k * cap : (k + 1) * cap] = jnp.where(live, picks_in[k, c : c + 1], 0.0)

    for k in range(SWEEPS):
        pl.when(has_next_s)(lambda: x_up(k).wait_send())
        pl.when(has_prev_s)(lambda: x_down(k).wait_send())
        pl.when(has_next_p)(lambda: y_up(k).wait_send())
        pl.when(has_prev_p)(lambda: y_down(k).wait_send())
    pl.when(has_next_p)(lambda: d_up().wait_send())
    pl.when(has_prev_p)(lambda: d_down().wait_send())
    for j in range(1, patches):
        point_first(j, True).wait_send()
        pull_first(j, True).wait_send()
        pick_copy(j, True).wait_send()
    for j in range(1, slabs):
        point_second(j, True).wait_send()
        pull_second(j, True).wait_send()


def shards(slabs, patches, *args):
    state, disp, elem = args[0], args[11], args[8]
    ex, ey, dof = state.shape
    comps, rows, cols = disp.shape
    cap = elem.shape[2] // patches
    sem = pltpu.SemaphoreType.DMA
    vmem = pl.BlockSpec(memory_space=pltpu.VMEM)
    return pl.pallas_call(
        functools.partial(kernel, slabs, patches),
        out_shape=(
            jax.ShapeDtypeStruct(state.shape, F32),
            jax.ShapeDtypeStruct(disp.shape, F32),
            jax.ShapeDtypeStruct((comps, 1, 1, elem.shape[2]), F32),
        ),
        in_specs=[vmem] * len(args),
        out_specs=(vmem, vmem, vmem),
        scratch_shapes=[
            pltpu.VMEM((SWEEPS, ex, ey, dof), BF16),
            pltpu.VMEM((SWEEPS, 2, ey, dof), BF16),
            pltpu.VMEM((SWEEPS, 2, ex, PACK, dof), BF16),
            pltpu.VMEM((2, comps, EDGE, cols), F32),
            pltpu.VMEM((slabs, patches, 1, cap), jnp.int32),
            pltpu.VMEM((slabs, patches, comps, cap), BF16),
            pltpu.VMEM((patches, comps, cap), BF16),
            pltpu.VMEM((patches, comps, cap), F32),
            pltpu.VMEM((patches, comps, cap), F32),
            pltpu.VMEM((patches, ex * ey, cap), BF16),
            pltpu.VMEM((slabs, rows, patches * cap), BF16),
            pltpu.VMEM((slabs, cols, patches * cap), BF16),
            pltpu.VMEM((comps, rows, cols), F32),
            sem((SWEEPS, 2)),
            sem((SWEEPS, 2)),
            sem((SWEEPS, 2)),
            sem((SWEEPS, 2)),
            sem((2,)),
            sem((2,)),
            sem((patches,)),
            sem((patches,)),
            sem((slabs,)),
            sem((slabs,)),
            sem((patches,)),
            sem((patches,)),
            sem((slabs,)),
            sem((slabs,)),
            sem((patches,)),
            sem((patches,)),
        ],
        compiler_params=pltpu.CompilerParams(collective_id=0, has_side_effects=True),
    )(*args)


def solution(mesh):
    return jax.shard_map(
        functools.partial(shards, mesh.shape["slab"], mesh.shape["patch"]),
        mesh=mesh,
        in_specs=(
            P("slab", "patch", None),
            P("slab", "patch", None),
            P("slab", "patch"),
            P(),
            P(),
            P(),
            P(),
            P(),
            P("slab", "patch", None),
            P("slab", "patch", None),
            P("slab", "patch", None),
            P(None, "patch", None),
            P("patch", None),
        ),
        out_specs=(
            P("slab", "patch", None),
            P(None, "patch", None),
            P(None, "slab", "patch", None),
        ),
        check_vma=False,
    )
```

time: 300 us -> 33.9 us (0.11)
  blocking collectives: 104 us -> 0 us
  waiting for transfers between devices: 80.6 us -> 0 us
  starting transfers between devices: 55.9 us -> 0 us
  Pallas kernels: 0 us -> 30.1 us
  local copies, waits for them, and re-layouts: 20.3 us -> 2.91 us
  other arithmetic: 16.7 us -> 0 us
  between operations: 14.5 us -> 0.65 us
  matrix products: 7.25 us -> 0 us
    all_gather x1 -> x0, blocking collectives: 104 us -> none  [shards(): whole = lax.all_gather(flat_net, 'patch', axis=1, tiled=True)]
    psum x1 -> x0, waiting for transfers between devices: 73.6 us -> none  [shards(): loads = lax.psum(local, 'slab')]
    ppermute x16 -> x0, starting transfers between devices: 46.1 us -> none  [the longest x8 35.8 us: with_halo(): lax.ppermute(tail, axis, [(i, (i + 1) % count) for i in range(ends)])]
    pallas_call x0 -> x1, Pallas kernels: none -> 30.1 us  [shards(): pl.pallas_call(functools.partial(kernel, slabs, patches), out_shape=(jax....]
    gather x2 -> x0, local copies, waits for them, and re-layouts: 12.5 us -> none  [the longest x1 8.57 us: shards(): picked = whole[:, (owner_ids * cells + points).reshape(-1)]]
    all_to_all x2 -> x0, starting transfers between devices: 9.77 us -> none  [the longest x1 6.5 us: shards(): lax.all_to_all(pull, 'patch', split_axis=0, concat_axis=0, tiled=True)]
    scatter-add x1 -> x0, other arithmetic: 8.21 us -> none  [shards(): local.at[:, got_points.reshape(-1)]]
    dot_general x10 -> x0, matrix products: 7.25 us -> none  [the longest x3 2.61 us: shards(): jnp.dot(residue.reshape(-1, width), block_inverse, preferred_element_type...]
  transfers between devices with their start and end apart: 19 -> 0, of which waited for: 6 -> 0; matrix products, arithmetic and copies ran while one was open for 10% -> 0% of each run, Pallas kernels for 0% -> 0%
where the time goes in v1:
time: 33.9 us; the launch traced here: 33.6 us
  Pallas kernels  30.1 us (89%)
  local copies, waits for them, and re-layouts  2.91 us (9%)
  between operations  0.65 us (2%)
    pallas_call x1, Pallas kernels, shards(): pl.pallas_call(functools.partial(kernel, slabs, patches), out_shape=(jax....  30.1 us
    unnamed x7, local copies, waits for them, and re-layouts  2.91 us

profile of v1, /device:TPU:0, one launch (start us, length us, event | category | flops | bytes accessed | tf_op | source)
XLA Modules:
  0.0 33.6 jit_solution(2089338756488546530)
XLA Ops:
  0.6 30.1 %shard_map.148 = (f32[2,64,256]{2,1,0:T(8,128)}, f32[3,64,128]{2,1,0:T(8,128)}, f32[3,1,1,1024]{3,2,1,0:T(1,128)}) custom-call(f32[2,64,256]{2,1,0:T(8,128)} %state_ref.1, f32[2,64,256]{2,1,0:T(8,128)} %rhs_ref.1, f32[2,64]{1,0:T(2,128)} %scale_ref.1, bf16[256,256]{1,0:T(8,128)(2,1)} %matrix_ref.1, bf16[256,256]{1,0:T(8,128)(2,1)} %cx_ref.1, ...), custom_call_target="tpu_custom_call" | custom-call | tf_op jit(solution)/shard_map/pallas_call | solution.py:358
  30.7 0.0 copy-start
  30.7 1.6 %copy.19 = f32[2,64,256]{2,1,0:T(8,128)} copy(f32[2,64,256]{2,1,0:T(8,128)} %get-tuple-element.6) | data formatting | bytes 262144
  32.3 0.0 copy-done
  32.3 0.0 copy-start.1
  32.3 0.6 %copy.20 = f32[3,64,128]{2,1,0:T(8,128)} copy(f32[3,64,128]{2,1,0:T(8,128)S(1)} %copy-done) | data formatting | bytes 196608
  33.0 0.1 copy-done.1
  33.0 0.6 %copy.21 = f32[3,1,1,1024]{3,2,1,0:T(1,128)} copy(f32[3,1,1,1024]{3,2,1,0:T(1,128)S(1)} %copy-done.1) | data formatting | bytes 24576
Async XLA Ops:
  30.7 1.6 %copy-start = (f32[3,64,128]{2,1,0:T(8,128)S(1)}, f32[3,64,128]{2,1,0:T(8,128)}, u32[]{:S(2)}) copy-start(f32[3,64,128]{2,1,0:T(8,128)} %get-tuple-element.7) | copy-start | bytes 294916
  32.3 0.7 %copy-start.1 = (f32[3,1,1,1024]{3,2,1,0:T(1,128)S(1)}, f32[3,1,1,1024]{3,2,1,0:T(1,128)}, u32[]{:S(2)}) copy-start(f32[3,1,1,1024]{3,2,1,0:T(1,128)} %get-tuple-element.8) | copy-start | bytes 36868

commit v2 on v1

--- a/solution.py
+++ b/solution.py
@@ -10,6 +10,8 @@
 SWEEPS = 3
 PACK = 16
 EDGE = 8
+SPARE = 8 * 2**20
+LOAD_ORDER = (0, 2, 3, 1, 8, 10, 9, 11, 12, 5, 4, 6, 7)
 MESH = pl.DeviceIdType.MESH
 F32 = jnp.float32
 BF16 = jnp.bfloat16
@@ -45,55 +47,24 @@
     return 4.0 * x - (pltpu.roll(x, 1, 0) + pltpu.roll(x, rows - 1, 0) + left + right)
 
 
-def kernel(
-    slabs,
-    patches,
-    state_ref,
-    rhs_ref,
-    scale_ref,
-    matrix_ref,
-    cx_ref,
-    cy_ref,
-    inverse_ref,
-    traction_ref,
-    elem_ref,
-    point_ref,
-    count_ref,
-    disp_ref,
-    stiff_ref,
-    fluid_ref,
-    net_ref,
-    wall_ref,
-    vb,
-    halo_x,
-    halo_y,
-    halo_d,
-    points,
-    pulls,
-    pull_out,
-    picks_out,
-    picks_in,
-    onehot_elem,
-    onehot_row,
-    onehot_col,
-    kd_buf,
-    sx,
-    rx,
-    sy,
-    ry,
-    sd,
-    rd,
-    sp1,
-    rp1,
-    sp2,
-    rp2,
-    sq1,
-    rq1,
-    sq2,
-    rq2,
-    sw,
-    rw,
-):
+def kernel(slabs, patches, args, *refs):
+    hbm, refs = refs[:args], refs[args:]
+    (fluid_ref, net_ref, wall_ref), refs = refs[:3], refs[3:]
+    staged, refs = refs[:args], refs[args:]
+    (state_ref, rhs_ref, scale_ref, matrix_ref, cx_ref, cy_ref, inverse_ref, traction_ref) = staged[:8]
+    (elem_ref, point_ref, count_ref, disp_ref, stiff_ref) = staged[8:]
+    (vb, halo_x, halo_y, halo_d, points, pulls, pull_out, picks_out, picks_in) = refs[:9]
+    (onehot_elem, onehot_row, onehot_col, rest_buf, gain_buf) = refs[9:14]
+    (load_sem, sx, rx, sy, ry, sd, rd, sp1, rp1, sp2, rp2, sq1, rq1, sq2, rq2, sw, rw, near_sem) = refs[14:]
+
+    loads_in = [pltpu.make_async_copy(hbm[n], staged[n], load_sem.at[n]) for n in range(args)]
+    for n in LOAD_ORDER:
+        loads_in[n].start()
+
+    def ready(*names):
+        for n in names:
+            loads_in[n].wait()
+
     s = lax.axis_index("slab")
     p = lax.axis_index("patch")
     ex, ey, dof = state_ref.shape
@@ -106,11 +77,33 @@
     def patch_peer(j):
         return lax.rem(p + j, patches)
 
+    def slab_sides(reach, semaphore):
+        @pl.when(s >= reach)
+        def _():
+            pl.semaphore_signal(semaphore, inc=1, device_id=(s - reach, p), device_id_type=MESH)
+
+        @pl.when(s + reach < slabs)
+        def _():
+            pl.semaphore_signal(semaphore, inc=1, device_id=(s + reach, p), device_id_type=MESH)
+
+    def slab_count(reach):
+        return jnp.where(s >= reach, 1, 0) + jnp.where(s + reach < slabs, 1, 0)
+
+    reaches = []
+    while 2 ** (len(reaches) + 1) < slabs - 1:
+        reaches.append(2 ** (len(reaches) + 1))
+
+    def near_signal(n):
+        slab_sides(reaches[n], near_sem.at[n])
+
+    def near_wait(n):
+        pl.semaphore_wait(near_sem.at[n], slab_count(reaches[n]))
+
     barrier = pltpu.get_barrier_semaphore()
-    for j in range(1, slabs):
-        pl.semaphore_signal(barrier, inc=1, device_id=(slab_peer(j), p), device_id_type=MESH)
     for j in range(1, patches):
         pl.semaphore_signal(barrier, inc=1, device_id=(s, patch_peer(j)), device_id_type=MESH)
+    slab_sides(1, barrier)
+    awaited = patches - 1 + slab_count(1)
 
     def remote(src, dst, send, recv, target):
         return pltpu.make_async_remote_copy(
@@ -178,6 +171,7 @@
         pl.when(has_next_p)(lambda: y_up(k).start())
         pl.when(has_prev_p)(lambda: y_down(k).start())
 
+    ready(2)
     scales = [column(scale_ref[i : i + 1, :]) for i in range(ex)]
     inverses = [1.0 / x for x in scales]
 
@@ -204,22 +198,28 @@
         first = jnp.where(has_prev_p, 0, EDGE)
         last = jnp.where(has_next_p, total, EDGE + rows)
         valid = (line >= first) & (line < last)
+        gain = 1.0 / (36.0 * stiff_ref[...])
+        gain_buf[...] = gain
         for c in range(comps):
             field = jnp.concatenate([halo_d[0, c], disp_ref[c], halo_d[1, c]], axis=0)
             field = jnp.where(valid, field, 0.0)
             bend = jnp.where(valid, laplace(field), 0.0)
             full = (laplace(bend) + 4.0 * bend)[EDGE : EDGE + rows]
-            kd_buf[c] = stiff_ref[...] * full
-
+            rest_buf[c] = disp_ref[c] - stiff_ref[...] * full * gain
+
+    ready(0)
     v = state_ref[...]
     for k in range(SWEEPS):
         rounded = v.astype(BF16)
         vb[k] = rounded
         if k > 0:
             send_halos(k)
+        if k == 0:
+            ready(3, 1)
         own = dot(rounded.reshape(ex * ey, dof), matrix_ref[...]).reshape(ex, ey, dof)
         base = [rhs_ref[i] - scales[i] * own[i] for i in range(ex)]
         if k == 0:
+            ready(8, 9, 10)
             for owner in range(patches):
                 elem = elem_ref[0, :, owner * cap : (owner + 1) * cap]
                 hit = (lax.broadcasted_iota(jnp.int32, (ex * ey, cap), 0) == elem) & lives(owner)
@@ -230,27 +230,30 @@
                 def _():
                     points[s, owner] = point_ref[0, :, owner * cap : (owner + 1) * cap]
 
-            pl.semaphore_wait(barrier, slabs - 1 + patches - 1)
+            pl.semaphore_wait(barrier, awaited)
             send_halos(0)
             for j in range(1, patches):
                 point_first(j, True).start()
+            ready(11, 12)
             pl.when(has_next_p)(lambda: d_up().start())
             pl.when(has_prev_p)(lambda: d_down().start())
+            ready(5, 4, 6, 7)
         if k == 1:
+            if reaches:
+                near_wait(0)
+                if len(reaches) > 1:
+                    near_signal(1)
             for j in range(1, patches):
                 point_first(j, False).wait_recv()
+            build_points(s)
+        if k == 2:
+            for n in range(1, len(reaches)):
+                near_wait(n)
+                if n + 1 < len(reaches):
+                    near_signal(n + 1)
             for j in range(1, slabs):
                 point_second(j, True).start()
-            build_points(s)
             shell()
-        if k == 2:
-
-            def arrive(j, carry):
-                point_second(j, False).wait_recv()
-                build_points(slab_peer(j))
-                return carry
-
-            lax.fori_loop(1, slabs, arrive, 0)
 
         wide = rounded.astype(F32)
         pl.when(has_prev_p)(lambda: y_up(k).wait_recv())
@@ -268,6 +271,8 @@
         side_y = dot(jnp.concatenate(along_y, axis=0), cy_ref[...])
         pl.when(has_prev_s)(lambda: x_up(k).wait_recv())
         pl.when(has_next_s)(lambda: x_down(k).wait_recv())
+        if k == 0 and reaches:
+            near_signal(0)
         low = jnp.where(has_prev_s, halo_x[k, 0].astype(F32), 0.0)
         high = jnp.where(has_next_s, halo_x[k, 1].astype(F32), 0.0)
         along_x = []
@@ -303,6 +308,12 @@
             acc = acc + dot_nt(scaled, onehot_col[slab, :, span])
         return acc
 
+    def arrive(j, carry):
+        point_second(j, False).wait_recv()
+        build_points(slab_peer(j))
+        return carry
+
+    lax.fori_loop(1, slabs, arrive, 0)
     acc = scatter(s, jnp.zeros((comps * rows, cols), F32))
 
     def gathered(j, acc):
@@ -311,8 +322,7 @@
 
     acc = lax.fori_loop(1, slabs, gathered, acc)
     loads = acc.reshape(comps, rows, cols)
-    gain = 1.0 / (36.0 * stiff_ref[...])
-    fresh = [disp_ref[c] + (loads[c] - kd_buf[c]) * gain for c in range(comps)]
+    fresh = [rest_buf[c] + loads[c] * gain_buf[...] for c in range(comps)]
     narrow = jnp.concatenate([x.astype(BF16) for x in fresh], axis=0)
     for k in range(patches):
         span = pl.ds(k * cap, cap)
@@ -348,6 +358,14 @@
         pull_second(j, True).wait_send()
 
 
+def deliver(*refs):
+    copies = [pltpu.make_async_copy(refs[n], refs[n + 3], refs[6].at[n]) for n in range(3)]
+    for copy in copies:
+        copy.start()
+    for copy in copies:
+        copy.wait()
+
+
 def shards(slabs, patches, *args):
     state, disp, elem = args[0], args[11], args[8]
     ex, ey, dof = state.shape
@@ -355,16 +373,18 @@
     cap = elem.shape[2] // patches
     sem = pltpu.SemaphoreType.DMA
     vmem = pl.BlockSpec(memory_space=pltpu.VMEM)
-    return pl.pallas_call(
-        functools.partial(kernel, slabs, patches),
+    hot_bytes = slabs * patches * cap * (rows + cols) * 2
+    outs = pl.pallas_call(
+        functools.partial(kernel, slabs, patches, len(args)),
         out_shape=(
             jax.ShapeDtypeStruct(state.shape, F32),
             jax.ShapeDtypeStruct(disp.shape, F32),
             jax.ShapeDtypeStruct((comps, 1, 1, elem.shape[2]), F32),
         ),
-        in_specs=[vmem] * len(args),
+        in_specs=[pl.BlockSpec(memory_space=pltpu.HBM)] * len(args),
         out_specs=(vmem, vmem, vmem),
-        scratch_shapes=[
+        scratch_shapes=[pltpu.VMEM(x.shape, x.dtype) for x in args]
+        + [
             pltpu.VMEM((SWEEPS, ex, ey, dof), BF16),
             pltpu.VMEM((SWEEPS, 2, ey, dof), BF16),
             pltpu.VMEM((SWEEPS, 2, ex, PACK, dof), BF16),
@@ -378,6 +398,8 @@
             pltpu.VMEM((slabs, rows, patches * cap), BF16),
             pltpu.VMEM((slabs, cols, patches * cap), BF16),
             pltpu.VMEM((comps, rows, cols), F32),
+            pltpu.VMEM((rows, cols), F32),
+            sem((len(args),)),
             sem((SWEEPS, 2)),
             sem((SWEEPS, 2)),
             sem((SWEEPS, 2)),
@@ -394,9 +416,17 @@
             sem((slabs,)),
             sem((patches,)),
             sem((patches,)),
+            pltpu.SemaphoreType.REGULAR((max(slabs.bit_length(), 1),)),
         ],
         compiler_params=pltpu.CompilerParams(collective_id=0, has_side_effects=True),
     )(*args)
+    return pl.pallas_call(
+        deliver,
+        out_shape=tuple(jax.ShapeDtypeStruct(x.shape, x.dtype) for x in outs),
+        in_specs=[vmem] * 3,
+        out_specs=(pl.BlockSpec(memory_space=pltpu.HBM),) * 3,
+        scratch_shapes=[sem((3,))],
+    )(*outs)
 
 
 def solution(mesh):

time: 33.9 us -> 30.4 us (0.90)
  local copies, waits for them, and re-layouts: 2.91 us -> 0 us
  Pallas kernels: 30.1 us -> 29.6 us
    unnamed x7 -> x0, local copies, waits for them, and re-layouts: 2.91 us -> none
    pallas_call x1 -> x2, Pallas kernels: 30.1 us -> 29.6 us  [the longest x1 27.9 us: shards(): pl.pallas_call(functools.partial(kernel, slabs, patches, len(args)), out_...]
where the time goes in v2:
time: 30.4 us; the launch traced here: 30.2 us
  Pallas kernels  29.6 us (97%)
  between operations  0.64 us (2%)
    pallas_call x1, Pallas kernels, shards(): pl.pallas_call(functools.partial(kernel, slabs, patches, len(args)), out_...  27.9 us
    pallas_call x1, Pallas kernels, shards(): pl.pallas_call(deliver, out_shape=tuple((jax.ShapeDtypeStruct(x.shape, x....  1.66 us

profile of v2, /device:TPU:0, one launch (start us, length us, event | category | flops | bytes accessed | tf_op | source)
XLA Modules:
  0.0 30.2 jit_solution(5291540954155538353)
XLA Ops:
  0.6 27.9 %shard_map.148 = (f32[2,64,256]{2,1,0:T(8,128)}, f32[3,64,128]{2,1,0:T(8,128)}, f32[3,1,1,1024]{3,2,1,0:T(1,128)}) custom-call(f32[2,64,256]{2,1,0:T(8,128)} %refs_0_.1, f32[2,64,256]{2,1,0:T(8,128)} %refs_1_.1, f32[2,64]{1,0:T(2,128)} %refs_2_.1, bf16[256,256]{1,0:T(8,128)(2,1)} %refs_3_.1, bf16[256,256]{1,0:T(8,128)(2,1)} %refs_4_.1, ...), custom_call_target="tpu_custom_call" | custom-call | tf_op jit(solution)/shard_map/pallas_call | solution.py:377
  28.6 1.7 %shard_map.149 = (f32[2,64,256]{2,1,0:T(8,128)}, f32[3,64,128]{2,1,0:T(8,128)}, f32[3,1,1,1024]{3,2,1,0:T(1,128)}) custom-call(f32[2,64,256]{2,1,0:T(8,128)} %get-tuple-element.6.refs_0_, f32[3,64,128]{2,1,0:T(8,128)} %get-tuple-element.7.refs_1_, f32[3,1,1,1024]{3,2,1,0:T(1,128)} %get-tuple-element.8.refs_2_), custom_call_target="tpu_custom_call" | custom-call | tf_op jit(solution)/shard_map/pallas_call | solution.py:423
